TPU v7x, 256 devices: a whole 4x4x8 slice. The times are simulated.
256 devices in a mesh: grp: 8 (over x, core), seq: 32 (over z, y).
Axes of the slice: x: 4, y: 4, z: 8, core: 2. Of those that a mesh axis runs over, the one named last changes fastest.
Arguments:
- queries: bfloat16 [8, 3, 32, 128, 512], P('grp', None, 'seq'), may hold values from -120 to 120
- key_input: bfloat16 [8, 3, 32, 128, 512], P('grp', None, 'seq'), may hold values from -8 to 8
- value_input: bfloat16 [8, 3, 32, 128, 512], P('grp', None, 'seq'), may hold values from -6 to 6
- grad_output: bfloat16 [8, 3, 32, 128, 512], P('grp', None, 'seq'), may hold values from -6 to 6
- block_lists: int32 [768, 16], replicated, may hold values from -1 to 767, as said below
- block_flags: int32 [768, 16], replicated, may hold values from 0 to 1, as said below
Outputs:
- attended: bfloat16 [8, 3, 32, 128, 512], P('grp', None, 'seq')
- grad_queries: bfloat16 [8, 3, 32, 128, 512], P('grp', None, 'seq')
- grad_keys: bfloat16 [8, 3, 32, 128, 512], P('grp', None, 'seq')
- grad_values: bfloat16 [8, 3, 32, 128, 512], P('grp', None, 'seq')
Inputs may be any that keep to these rules, and one draw needn't show every extreme that they name: `block_lists`: entry 0 of row t is t itself; the other used entries of a row are distinct tiles u < t, each either in the same block of 96 tiles as t, or in an earlier block with u % 32 == t % 32; used entries come first and -1 fills the rest. The 3 rows t = (a * 3 + b) * 32 + c that share a and c name together at most one tile of the form (a2 * 3 + b2) * 32 + c2 for each pair (a2, c2) other than (a, c). block_flags[t, 0] is 1 for every t; a flag whose list entry is -1 has no effect.
All inputs are finite; a program needn't handle non-finite values.
Results may differ from a plain program's by a relative error of at most 0.029.
Values may be sent and summed in bfloat16 or wider, within the bound.
No kernel may reach another device: no remote copies, remote signals or barrier semaphores. Data moves between devices by JAX's collectives and lax.ppermute only.
A program may use at most 256 MiB of HBM per device.

v0:
```python
import jax
import jax.numpy as jnp
from jax import lax
from jax.sharding import PartitionSpec as P

HEADS = 8
HEAD_DIM = 64
floor_score = -1e30


def locate(entry_ids, group_tiles, columns):
    safe_ids = jnp.maximum(entry_ids, 0)
    within = safe_ids % group_tiles
    return (safe_ids // group_tiles, within // columns, within % columns)


def per_device(queries, key_input, value_input, grad_output, block_lists, block_flags):
    tile_dev = queries.shape[1]
    tile_rows = queries.shape[3]
    width = queries.shape[4]
    entries = block_lists.shape[1]
    columns = lax.axis_size("seq")
    groups = lax.axis_size("grp")
    group_at = lax.axis_index("grp")
    column_at = lax.axis_index("seq")
    group_tiles = tile_dev * columns
    query_tiles = queries.reshape(tile_dev, tile_rows, width)
    key_tiles = key_input.reshape(tile_dev, tile_rows, width)
    value_tiles = value_input.reshape(tile_dev, tile_rows, width)
    grad_tiles = grad_output.reshape(tile_dev, tile_rows, width)
    ranks = jnp.arange(tile_dev, dtype=jnp.int32)
    column_ids = jnp.arange(columns, dtype=jnp.int32)
    group_ids = jnp.arange(groups, dtype=jnp.int32)
    my_tiles = (group_at * tile_dev + ranks) * columns + column_at
    my_lists = jnp.take(block_lists, my_tiles, axis=0)
    my_flags = jnp.take(block_flags, my_tiles, axis=0)
    present = my_lists >= 0
    owner_group, owner_rank, owner_column = locate(my_lists, group_tiles, columns)
    same_group = owner_group == group_at
    is_own = present & same_group & (owner_column == column_at)
    is_near = present & same_group & (owner_column != column_at)
    is_far = present & jnp.logical_not(same_group)
    group_rows = lax.dynamic_slice_in_dim(block_lists, group_at * group_tiles, group_tiles, 0)
    group_rows = group_rows.reshape(tile_dev, columns, entries)
    row_group, row_rank, row_column = locate(group_rows, group_tiles, columns)
    named_here = (group_rows >= 0) & (row_group == group_at) & (row_column == column_at)
    near_rank = jnp.max(jnp.where(named_here, row_rank, -1), axis=(0, 2))
    near_rank = jnp.where(column_ids == column_at, -1, near_rank)
    column_rows = jnp.take(
        block_lists.reshape(groups, tile_dev, columns, entries), column_at, axis=2
    )
    far_group, far_rank_all, far_column = locate(column_rows, group_tiles, columns)
    named_far = (column_rows >= 0) & (far_group == group_at) & (far_column == column_at)
    far_rank = jnp.max(jnp.where(named_far, far_rank_all, -1), axis=(1, 2))
    far_rank = jnp.where(group_ids == group_at, -1, far_rank)
    wanted = jnp.max(
        jnp.where(
            is_near[:, :, None] & (owner_column[:, :, None] == column_ids),
            owner_rank[:, :, None],
            -1,
        ),
        axis=(0, 1),
    )
    pieces = (
        lax.all_gather(key_tiles, "seq", axis=0, tiled=True),
        lax.all_gather(value_tiles, "seq", axis=0, tiled=True),
    )
    span_rows = pieces[0].shape[0]
    row_at = jnp.arange(span_rows, dtype=jnp.int32)
    select = (
        (row_at[None, :] // tile_dev == column_ids[:, None])
        & (row_at[None, :] % tile_dev == wanted[:, None])
    ).astype(jnp.bfloat16)
    new_keys = jnp.einsum("pn,ntw->ptw", select, pieces[0], preferred_element_type=jnp.float32)
    new_values = jnp.einsum("pn,ntw->ptw", select, pieces[1], preferred_element_type=jnp.float32)
    near_keys = new_keys.astype(jnp.bfloat16)
    near_values = new_values.astype(jnp.bfloat16)
    far_out = jnp.maximum(far_rank, 0)
    far_keys, far_values = (
        lax.all_to_all(
            jnp.take(key_tiles, far_out, axis=0), "grp", split_axis=0, concat_axis=0, tiled=True
        ),
        lax.all_to_all(
            jnp.take(value_tiles, far_out, axis=0), "grp", split_axis=0, concat_axis=0, tiled=True
        ),
    )
    own_slot = jnp.where(is_own, owner_rank, 0)
    near_slot = jnp.where(is_near, owner_column, 0)
    far_slot = jnp.where(is_far, owner_group, 0)
    own_pick = is_own[:, :, None, None]
    near_pick = is_near[:, :, None, None]
    far_pick = is_far[:, :, None, None]
    pair_width = 2 * HEAD_DIM
    score_scale = HEAD_DIM ** (-0.5)
    positions = jnp.arange(tile_rows)
    lower_mask = positions[None, :] <= positions[:, None]
    allowed = present[:, None, :, None] & (
        (my_flags == 0)[:, None, :, None] | lower_mask[None, :, None, :]
    )

    def spread(term, chosen_pick, slot, slots):
        total = jnp.zeros((slots, tile_rows, pair_width), jnp.float32)
        return total.at[slot].add(jnp.where(chosen_pick, term, 0.0)).astype(jnp.bfloat16)

    attended_parts = []
    query_parts = []
    own_key_parts = []
    near_key_parts = []
    far_key_parts = []
    own_value_parts = []
    near_value_parts = []
    far_value_parts = []
    for head_pair in range(HEADS // 2):
        start_col = head_pair * pair_width

        def columns_of(source):
            return source[..., start_col : start_col + pair_width]

        def fetch(own_source, near_source, far_source):
            from_own = jnp.take(columns_of(own_source), own_slot, axis=0)
            from_near = jnp.take(columns_of(near_source), near_slot, axis=0)
            from_far = jnp.take(columns_of(far_source), far_slot, axis=0)
            return jnp.where(own_pick, from_own, jnp.where(near_pick, from_near, from_far))

        key_block = fetch(key_tiles, near_keys, far_keys).reshape(
            tile_dev, entries, tile_rows, 2, HEAD_DIM
        )
        value_block = fetch(value_tiles, near_values, far_values).reshape(
            tile_dev, entries, tile_rows, 2, HEAD_DIM
        )
        query_block = columns_of(query_tiles).reshape(tile_dev, tile_rows, 2, HEAD_DIM)
        grad_block = columns_of(grad_tiles).reshape(tile_dev, tile_rows, 2, HEAD_DIM)
        scores = (
            jnp.einsum(
                "tihd,techd->thiec", query_block, key_block, preferred_element_type=jnp.float32
            )
            * score_scale
        )
        masked = jnp.where(allowed[:, None], scores, floor_score)
        row_top = jnp.max(masked, axis=(3, 4), keepdims=True)
        exponent = jnp.exp(masked - row_top)
        probs_exact = exponent / jnp.sum(exponent, axis=(3, 4), keepdims=True)
        probs = probs_exact.astype(jnp.bfloat16)
        attended_block = jnp.einsum(
            "thiec,techd->tihd", probs, value_block, preferred_element_type=jnp.float32
        ).astype(jnp.bfloat16)
        row_delta = jnp.sum(
            grad_block.astype(jnp.float32) * attended_block.astype(jnp.float32), axis=3
        )
        dprobs = jnp.einsum(
            "tihd,techd->thiec", grad_block, value_block, preferred_element_type=jnp.float32
        )
        dscores = (
            probs_exact * (dprobs - jnp.transpose(row_delta, (0, 2, 1))[..., None, None])
        ).astype(jnp.bfloat16)
        grad_query = (
            jnp.einsum("thiec,techd->tihd", dscores, key_block, preferred_element_type=jnp.float32)
            * score_scale
        )
        grad_key = (
            jnp.einsum(
                "thiec,tihd->techd", dscores, query_block, preferred_element_type=jnp.float32
            )
            * score_scale
        )
        grad_value = jnp.einsum(
            "thiec,tihd->techd", probs, grad_block, preferred_element_type=jnp.float32
        )
        grad_key = grad_key.reshape(tile_dev, entries, tile_rows, pair_width)
        grad_value = grad_value.reshape(tile_dev, entries, tile_rows, pair_width)
        attended_parts.append(attended_block.reshape(tile_dev, tile_rows, pair_width))
        query_parts.append(grad_query.astype(jnp.bfloat16).reshape(tile_dev, tile_rows, pair_width))
        own_key_parts.append(spread(grad_key, own_pick, own_slot, tile_dev))
        near_key_parts.append(spread(grad_key, near_pick, near_slot, columns))
        far_key_parts.append(spread(grad_key, far_pick, far_slot, groups))
        own_value_parts.append(spread(grad_value, own_pick, own_slot, tile_dev))
        near_value_parts.append(spread(grad_value, near_pick, near_slot, columns))
        far_value_parts.append(spread(grad_value, far_pick, far_slot, groups))

    def joined(parts):
        return jnp.concatenate(parts, axis=-1)

    near_back_keys, near_back_values = (
        lax.all_to_all(joined(near_key_parts), "seq", split_axis=0, concat_axis=0, tiled=True),
        lax.all_to_all(joined(near_value_parts), "seq", split_axis=0, concat_axis=0, tiled=True),
    )
    far_back_keys, far_back_values = (
        lax.all_to_all(joined(far_key_parts), "grp", split_axis=0, concat_axis=0, tiled=True),
        lax.all_to_all(joined(far_value_parts), "grp", split_axis=0, concat_axis=0, tiled=True),
    )
    near_onehot = (near_rank[None, :] == ranks[:, None]).astype(jnp.bfloat16)
    far_onehot = (far_rank[None, :] == ranks[:, None]).astype(jnp.bfloat16)

    def collect(own_part, near_back, far_back):
        total = own_part.astype(jnp.float32)
        total = total + jnp.einsum(
            "rp,ptw->rtw", near_onehot, near_back, preferred_element_type=jnp.float32
        )
        total = total + jnp.einsum(
            "rg,gtw->rtw", far_onehot, far_back, preferred_element_type=jnp.float32
        )
        return total.astype(jnp.bfloat16).reshape(1, tile_dev, 1, tile_rows, width)

    attended = joined(attended_parts).reshape(1, tile_dev, 1, tile_rows, width)
    grad_queries = joined(query_parts).reshape(1, tile_dev, 1, tile_rows, width)
    grad_keys = collect(joined(own_key_parts), near_back_keys, far_back_keys)
    grad_values = collect(joined(own_value_parts), near_back_values, far_back_values)
    return (attended, grad_queries, grad_keys, grad_values)


def solution(mesh):
    return jax.shard_map(
        per_device,
        mesh=mesh,
        in_specs=(
            P("grp", None, "seq", None, None),
            P("grp", None, "seq", None, None),
            P("grp", None, "seq", None, None),
            P("grp", None, "seq", None, None),
            P(),
            P(),
        ),
        out_specs=(
            P("grp", None, "seq", None, None),
            P("grp", None, "seq", None, None),
            P("grp", None, "seq", None, None),
            P("grp", None, "seq", None, None),
        ),
        check_vma=False,
    )
```

profile of v0, /device:TPU:1, one launch (start us, length us, event | category | flops | bytes accessed | tf_op | source)
XLA Modules:
  0.0 858.7 jit_solution(12798939972070502319)
XLA Ops:
  17.0 6.8 all-to-all-start
  29.0 10.0 %all-to-all-done = bf16[8,128,512]{2,1,0:T(8,128)(2,1)S(1)} async-done(((bf16[8,128,512]{2,1,0:T(8,128)(2,1)}), bf16[8,128,512]{2,1,0:T(8,128)(2,1)S(1)}, u32[]{:S(2)}, u32[]{:S(2)}) %all-to-all-start) | async-done | bytes 1048608 | tf_op jit(solution)/shard_map/all_to_all | solution.py:83
  39.0 5.0 all-to-all-start.1
  126.1 7.6 all-gather.5.cloned.1.call-done
  133.7 19.3 %fusion.26 = bf16[32,128,512]{2,0,1:T(8,128)(2,1)S(1)} fusion(bf16[1,96,1,128,512]{4,3,2,0,1:T(8,128)(2,1)} %all-gather.5.cloned.1.call-done, s32[96]{0:T(128)S(1)} %get-tuple-element.179, s32[96]{0:T(128)S(1)} %copy-done.72, s32[32]{0:T(128)S(1)} %select_reduce_fusion), kind=kOutput, calls=%fused_computation.121 | convolution fusion | flops 404759552 | bytes 16778112 | tf_op jit(solution)/shard_map/pn,ntw->ptw/dot_general | solution.py:75
  160.2 92.9 %all-gather.7.cloned.1.call-done = bf16[1,96,1,128,512]{4,3,2,0,1:T(8,128)(2,1)} async-done(((bf16[1,3,1,128,512]{4,3,2,0,1:T(8,128)(2,1)}), bf16[1,96,1,128,512]{4,3,2,0,1:T(8,128)(2,1)}) %all-gather.7.cloned.1.call-update) | async-done | bytes 12582928 | tf_op jit(solution)/shard_map/all_gather | solution.py:65
  253.1 19.1 %fusion.29 = bf16[32,128,512]{2,0,1:T(8,128)(2,1)S(1)} fusion(bf16[1,96,1,128,512]{4,3,2,0,1:T(8,128)(2,1)} %all-gather.7.cloned.1.call-done, s32[96]{0:T(128)S(1)} %get-tuple-element.179, s32[96]{0:T(128)S(1)} %copy-done.72, s32[32]{0:T(128)S(1)} %select_reduce_fusion), kind=kOutput, calls=%fused_computation.122 | convolution fusion | flops 404759552 | bytes 16778112 | tf_op jit(solution)/shard_map/pn,ntw->ptw/dot_general | solution.py:74
  316.8 8.7 %fusion.35 = (bf16[3,16,128,128]{2,3,1,0:T(8,128)(2,1)}, bf16[3,16,128,128]{2,3,1,0:T(8,128)(2,1)S(1)}, bf16[3,16,128,128]{2,3,1,0:T(8,128)(2,1)}, bf16[3,16,128,128]{2,3,1,0:T(8,128)(2,1)S(1)}) fusion(bf16[3,16,128,128]{2,3,1,0:T(8,128)(2,1)} %bitcast.460, bf16[3,16,128,128]{2,3,1,0:T(8,128)(2,1)} %copy.966, bf16[3,16,128,128]{2,3,1,0:T(8,128)(2,1)S(1)} %bitcast.452, ...), kind=kLoop, calls=%fused_computation.134 | loop fusion | flops 15728640 | bytes 25166064 | tf_op jit(solution)/shard_map/jit(_where)/select_n | solution.py:123
  331.0 4.9 fusion.39
  335.9 6.2 fusion.18
  342.2 6.1 fusion.11
  348.3 4.0 fusion.13
  385.5 4.8 fusion.9
  409.9 32.1 %bitcast_select_fusion.18 = (f32[3,16,128,128]{2,3,1,0:T(8,128)}, f32[3,16,128,128]{2,3,1,0:T(8,128)}, f32[3,16,128,128]{2,3,1,0:T(8,128)}, f32[3,16,128,128]{2,...) fusion(f32[3,16,128,2,64]{2,4,3,1,0:T(8,128)S(1)} %copy.1022, ...), kind=kLoop, calls=%fused_computation.106 | loop fusion | flops 18874368 | bytes 100663440 | tf_op jit(solution)/shard_map/jit(_where)/select_n | solution.py:103
  445.7 7.1 scatter_fusion.11
  452.8 3.6 copy.1032
  456.5 6.7 scatter_fusion.10
  463.9 3.6 copy.1031
  467.6 6.7 scatter_fusion.9
  478.7 6.7 scatter_fusion.8
  487.7 5.3 all-to-all-start.3
  495.4 6.7 scatter_fusion.23
  505.7 6.7 scatter_fusion.22
  513.2 3.7 copy.1055
  517.0 6.7 scatter_fusion.21
  528.0 6.7 scatter_fusion.20
  537.1 5.0 all-to-all-start.5
  544.8 6.7 scatter_fusion.7
  555.5 6.7 scatter_fusion.6
  567.2 6.7 scatter_fusion.5
  578.8 6.7 scatter_fusion.4
  589.3 5.8 all-to-all-start.2
  597.8 6.7 scatter_fusion.19
  608.5 6.7 scatter_fusion.18
  620.1 6.7 scatter_fusion.17
  631.8 6.7 scatter_fusion.16
  642.3 45.9 %all-to-all-done.2 = bf16[32,128,512]{2,1,0:T(8,128)(2,1)} async-done(((bf16[32,128,512]{2,1,0:T(8,128)(2,1)}), bf16[32,128,512]{2,1,0:T(8,128)(2,1)}, u32[]{:S(2)}, u32[]{:S(2)}) %all-to-all-start.2) | async-done | bytes 4194336 | tf_op jit(solution)/shard_map/all_to_all | solution.py:184
  688.3 9.9 %all-to-all-start.4 = ((bf16[32,128,512]{2,1,0:T(8,128)(2,1)}), bf16[32,128,512]{2,1,0:T(8,128)(2,1)}, u32[]{:S(2)}, u32[]{:S(2)}) async-start(bf16[32,128,512]{2,1,0:T(8,128)(2,1)} %pad_maximum_fusion.1), calls=%async_computation.4 | async-start | bytes 8388608 | tf_op jit(solution)/shard_map/all_to_all | solution.py:185
  719.1 10.2 %scatter_fusion.3 = f32[3,128,128]{2,1,0:T(8,128)} fusion(f32[3,128,128]{2,1,0:T(8,128)} %broadcast.258.clone, s32[48]{0:T(128)S(1)} %copy-done.41, f32[48,128,128]{2,1,0:T(8,128)S(1)} %copy.1023), kind=kCustom, calls=%fused_computation.31 | custom fusion | flops 786432 | bytes 9437376 | tf_op jit(solution)/shard_map/scatter-add | solution.py:103
  733.4 10.2 %scatter_fusion.2 = f32[3,128,128]{2,1,0:T(8,128)} fusion(f32[3,128,128]{2,1,0:T(8,128)} %broadcast.258.clone.1, s32[48]{0:T(128)S(1)} %copy-done.41, f32[48,128,128]{2,1,0:T(8,128)S(1)} %copy.1020), kind=kCustom, calls=%fused_computation.30 | custom fusion | flops 786432 | bytes 9437376 | tf_op jit(solution)/shard_map/scatter-add | solution.py:103
  747.6 10.2 %scatter_fusion.1 = f32[3,128,128]{2,1,0:T(8,128)} fusion(f32[3,128,128]{2,1,0:T(8,128)} %broadcast.258.clone.2, s32[48]{0:T(128)S(1)} %copy-done.41, f32[48,128,128]{2,1,0:T(8,128)S(1)} %copy.1017), kind=kCustom, calls=%fused_computation.29 | custom fusion | flops 786432 | bytes 9437376 | tf_op jit(solution)/shard_map/scatter-add | solution.py:103
  761.8 10.2 %scatter_fusion = f32[3,128,128]{2,1,0:T(8,128)} fusion(f32[3,128,128]{2,1,0:T(8,128)} %broadcast.258.clone.3, s32[48]{0:T(128)S(1)} %copy-done.41, f32[48,128,128]{2,1,0:T(8,128)S(1)} %copy.1014), kind=kCustom, calls=%fused_computation.28 | custom fusion | flops 786432 | bytes 9437376 | tf_op jit(solution)/shard_map/scatter-add | solution.py:103
  776.7 10.2 %scatter_fusion.15 = f32[3,128,128]{2,1,0:T(8,128)} fusion(f32[3,128,128]{2,1,0:T(8,128)} %broadcast.258.clone.4, s32[48]{0:T(128)S(1)} %copy-done.41, f32[48,128,128]{2,1,0:T(8,128)S(1)} %copy.1047), kind=kCustom, calls=%fused_computation.43 | custom fusion | flops 786432 | bytes 9437376 | tf_op jit(solution)/shard_map/scatter-add | solution.py:103
  791.0 10.2 %scatter_fusion.14 = f32[3,128,128]{2,1,0:T(8,128)} fusion(f32[3,128,128]{2,1,0:T(8,128)} %broadcast.258.clone.5, s32[48]{0:T(128)S(1)} %copy-done.41, f32[48,128,128]{2,1,0:T(8,128)S(1)} %copy.1044), kind=kCustom, calls=%fused_computation.42 | custom fusion | flops 786432 | bytes 9437376 | tf_op jit(solution)/shard_map/scatter-add | solution.py:103
  805.8 10.2 %scatter_fusion.13 = f32[3,128,128]{2,1,0:T(8,128)} fusion(f32[3,128,128]{2,1,0:T(8,128)} %broadcast.258.clone.6, s32[48]{0:T(128)S(1)} %copy-done.41, f32[48,128,128]{2,1,0:T(8,128)S(1)} %copy.1041), kind=kCustom, calls=%fused_computation.41 | custom fusion | flops 786432 | bytes 9437376 | tf_op jit(solution)/shard_map/scatter-add | solution.py:103
  820.9 10.2 %scatter_fusion.12 = f32[3,128,128]{2,1,0:T(8,128)} fusion(f32[3,128,128]{2,1,0:T(8,128)} %broadcast.258.clone.7, s32[48]{0:T(128)S(1)} %copy-done.41, f32[48,128,128]{2,1,0:T(8,128)S(1)} %copy.1038), kind=kCustom, calls=%fused_computation.40 | custom fusion | flops 786432 | bytes 9437376 | tf_op jit(solution)/shard_map/scatter-add | solution.py:103
  839.7 4.6 fusion.24
  845.6 4.6 fusion.22
  (383 shorter events, 333.4 us)
Async XLA Ops:
  7.2 5.2 copy-start.12
  7.2 126.5 %all-gather.5.cloned.1.call-start = ((), (), s32[]{:S(2)}) async-start(), calls=%async_computation.6 | async-start | bytes 12976128 | tf_op jit(solution)/shard_map/all_gather | solution.py:66
  7.9 245.2 %all-gather.7.cloned.1.call-start = ((), (), s32[]{:S(2)}) async-start(), calls=%async_computation.7 | async-start | bytes 12976128 | tf_op jit(solution)/shard_map/all_gather | solution.py:65
  14.0 9.8 %copy-start.56 = (s32[768,16]{0,1:T(8,128)S(1)}, s32[768,16]{0,1:T(8,128)}, u32[]{:S(2)}) copy-start(s32[768,16]{0,1:T(8,128)} %param.20) | copy-start | bytes 147460
  14.0 10.0 %copy-start.65 = (s32[768,16]{0,1:T(8,128)S(1)}, s32[768,16]{0,1:T(8,128)}, u32[]{:S(2)}) copy-start(s32[768,16]{0,1:T(8,128)} %param.21) | copy-start | bytes 147460
  14.0 13.3 %copy-start.13 = (bf16[1,3,1,128,512]{4,3,2,1,0:T(8,128)(2,1)S(1)}, bf16[1,3,1,128,512]{4,3,2,1,0:T(8,128)(2,1)}, u32[]{:S(2)}) copy-start(bf16[1,3,1,128,512]{4,3,2,1,0:T(8,128)(2,1)} %param.17) | copy-start | bytes 1179652
  17.0 10.4 %copy-start.51 = (bf16[1,3,1,128,512]{4,3,2,1,0:T(8,128)(2,1)S(1)}, bf16[1,3,1,128,512]{4,3,2,1,0:T(8,128)(2,1)}, u32[]{:S(2)}) copy-start(bf16[1,3,1,128,512]{4,3,2,1,0:T(8,128)(2,1)} %param.19) | copy-start | bytes 1179652
  17.0 11.2 %copy-start.52 = (bf16[1,3,1,128,512]{4,3,2,1,0:T(8,128)(2,1)S(1)}, bf16[1,3,1,128,512]{4,3,2,1,0:T(8,128)(2,1)}, u32[]{:S(2)}) copy-start(bf16[1,3,1,128,512]{4,3,2,1,0:T(8,128)(2,1)} %param.16) | copy-start | bytes 1179652
  17.0 21.9 %all-to-all-start = ((bf16[8,128,512]{2,1,0:T(8,128)(2,1)}), bf16[8,128,512]{2,1,0:T(8,128)(2,1)S(1)}, u32[]{:S(2)}, u32[]{:S(2)}) async-start(bf16[8,128,512]{2,1,0:T(8,128)(2,1)} %get-tuple-element.167), calls=%async_computation | async-start | bytes 2097152 | tf_op jit(solution)/shard_map/all_to_all | solution.py:83
  26.0 302.3 %copy-start.68 = (pred[3,16]{1,0:T(4,128)(4,1)}, pred[3,16]{1,0:T(4,128)(4,1)S(1)}, u32[]{:S(2)}) copy-start(pred[3,16]{1,0:T(4,128)(4,1)S(1)} %get-tuple-element.61) | copy-start | bytes 148
  26.5 301.8 %copy-start.66 = (pred[3,16]{1,0:T(4,128)(4,1)}, pred[3,16]{1,0:T(4,128)(4,1)S(1)}, u32[]{:S(2)}) copy-start(pred[3,16]{1,0:T(4,128)(4,1)S(1)} %get-tuple-element.69) | copy-start | bytes 148
  39.0 11.1 %copy-start.24 = (bf16[8,128,512]{2,1,0:T(8,128)(2,1)}, bf16[8,128,512]{2,1,0:T(8,128)(2,1)S(1)}, u32[]{:S(2)}) copy-start(bf16[8,128,512]{2,1,0:T(8,128)(2,1)S(1)} %all-to-all-done) | copy-start | bytes 3145732
  39.0 53.7 %all-to-all-start.1 = ((bf16[8,128,512]{2,1,0:T(8,128)(2,1)}), bf16[8,128,512]{2,1,0:T(8,128)(2,1)}, u32[]{:S(2)}, u32[]{:S(2)}) async-start(bf16[8,128,512]{2,1,0:T(8,128)(2,1)} %get-tuple-element.166), calls=%async_computation.1 | async-start | bytes 2097152 | tf_op jit(solution)/shard_map/all_to_all | solution.py:80
  46.1 38.6 %copy-start.42 = (s32[48]{0:T(128)}, s32[48]{0:T(128)S(1)}, u32[]{:S(2)}) copy-start(s32[48]{0:T(128)S(1)} %reshape.872) | copy-start | bytes 580
  64.1 261.5 %copy-start.36 = (bf16[3,128,128]{1,2,0:T(8,128)(2,1)}, bf16[3,128,128]{1,2,0:T(8,128)(2,1)S(1)}, u32[]{:S(2)}) copy-start(bf16[3,128,128]{1,2,0:T(8,128)(2,1)S(1)} %copy.972) | copy-start | bytes 294916
  75.9 8.1 copy-start.53
  75.9 9.0 %copy-start.73 = (pred[3,16]{1,0:T(4,128)(4,1)S(1)}, pred[3,16]{1,0:T(4,128)(4,1)}, u32[]{:S(2)}) copy-start(pred[3,16]{1,0:T(4,128)(4,1)} %get-tuple-element.165) | copy-start | bytes 148
  76.7 6.5 copy-start.54
  121.4 12.3 %copy-start.72 = (s32[96]{0:T(128)S(1)}, s32[96]{0:T(128)}, u32[]{:S(2)}) copy-start(s32[96]{0:T(128)} %get-tuple-element.180) | copy-start | bytes 1156
  331.0 4.9 copy-start.46
  335.9 6.3 copy-start.14
  335.9 6.3 copy-start.15
  335.9 6.3 copy-start.29
  335.9 6.3 copy-start.47
  362.0 28.3 %copy-start.4 = (bf16[3,2,128,16,128]{2,4,3,1,0:T(8,128)(2,1)}, bf16[3,2,128,16,128]{2,4,3,1,0:T(8,128)(2,1)S(1)}, u32[]{:S(2)}) copy-start(bf16[3,2,128,16,128]{2,4,3,1,0:T(8,128)(2,1)S(1)} %fusion.6) | copy-start | bytes 9437188
  370.4 36.5 %copy-start.5 = (bf16[3,2,128,16,128]{2,4,3,1,0:T(8,128)(2,1)}, bf16[3,2,128,16,128]{2,4,3,1,0:T(8,128)(2,1)S(1)}, u32[]{:S(2)}) copy-start(bf16[3,2,128,16,128]{2,4,3,1,0:T(8,128)(2,1)S(1)} %fusion.7) | copy-start | bytes 9437188
  373.3 6.5 slice-start
  379.9 23.9 %copy-start.6 = (bf16[3,2,128,16,128]{2,4,3,1,0:T(8,128)(2,1)}, bf16[3,2,128,16,128]{2,4,3,1,0:T(8,128)(2,1)S(1)}, u32[]{:S(2)}) copy-start(bf16[3,2,128,16,128]{2,4,3,1,0:T(8,128)(2,1)S(1)} %fusion.8) | copy-start | bytes 9437188
  385.5 4.8 copy-start.39
  390.3 10.4 %copy-start.7 = (bf16[3,2,128,16,128]{2,4,3,1,0:T(8,128)(2,1)}, bf16[3,2,128,16,128]{2,4,3,1,0:T(8,128)(2,1)S(1)}, u32[]{:S(2)}) copy-start(bf16[3,2,128,16,128]{2,4,3,1,0:T(8,128)(2,1)S(1)} %fusion.9) | copy-start | bytes 9437188
  485.4 7.6 copy-start.11
  487.7 49.4 %all-to-all-start.3 = ((bf16[8,128,512]{2,1,0:T(8,128)(2,1)}), bf16[8,128,512]{2,1,0:T(8,128)(2,1)}, u32[]{:S(2)}, u32[]{:S(2)}) async-start(bf16[8,128,512]{2,1,0:T(8,128)(2,1)} %pad_maximum_fusion.2), calls=%async_computation.3 | async-start | bytes 2097152 | tf_op jit(solution)/shard_map/all_to_all | solution.py:188
  534.8 7.4 copy-start.10
  537.1 52.2 %all-to-all-start.5 = ((bf16[8,128,512]{2,1,0:T(8,128)(2,1)}), bf16[8,128,512]{2,1,0:T(8,128)(2,1)}, u32[]{:S(2)}, u32[]{:S(2)}) async-start(bf16[8,128,512]{2,1,0:T(8,128)(2,1)} %pad_maximum_fusion.3), calls=%async_computation.5 | async-start | bytes 2097152 | tf_op jit(solution)/shard_map/all_to_all | solution.py:189
  589.3 5.8 copy-start.9
  589.3 98.9 %all-to-all-start.2 = ((bf16[32,128,512]{2,1,0:T(8,128)(2,1)}), bf16[32,128,512]{2,1,0:T(8,128)(2,1)}, u32[]{:S(2)}, u32[]{:S(2)}) async-start(bf16[32,128,512]{2,1,0:T(8,128)(2,1)} %pad_maximum_fusion), calls=%async_computation.2 | async-start | bytes 8388608 | tf_op jit(solution)/shard_map/all_to_all | solution.py:184
  642.3 57.0 %copy-start.57 = (bf16[3,2,64,128]{3,2,1,0:T(8,128)(2,1)S(1)}, bf16[3,2,64,128]{3,2,1,0:T(8,128)(2,1)}, u32[]{:S(2)}) copy-start(bf16[3,2,64,128]{3,2,1,0:T(8,128)(2,1)} %get-tuple-element.172) | copy-start | bytes 294916
  642.3 57.7 %copy-start.58 = (bf16[3,2,64,128]{3,2,1,0:T(8,128)(2,1)S(1)}, bf16[3,2,64,128]{3,2,1,0:T(8,128)(2,1)}, u32[]{:S(2)}) copy-start(bf16[3,2,64,128]{3,2,1,0:T(8,128)(2,1)} %get-tuple-element.174) | copy-start | bytes 294916
  642.3 58.5 %copy-start.59 = (bf16[3,2,64,128]{3,2,1,0:T(8,128)(2,1)S(1)}, bf16[3,2,64,128]{3,2,1,0:T(8,128)(2,1)}, u32[]{:S(2)}) copy-start(bf16[3,2,64,128]{3,2,1,0:T(8,128)(2,1)} %get-tuple-element.176) | copy-start | bytes 294916
  642.3 59.3 %copy-start.60 = (bf16[3,2,64,128]{3,2,1,0:T(8,128)(2,1)S(1)}, bf16[3,2,64,128]{3,2,1,0:T(8,128)(2,1)}, u32[]{:S(2)}) copy-start(bf16[3,2,64,128]{3,2,1,0:T(8,128)(2,1)} %get-tuple-element.178) | copy-start | bytes 294916
  642.3 60.0 %copy-start.3 = (bf16[3,16,128,128]{2,3,1,0:T(8,128)(2,1)S(1)}, bf16[3,16,128,128]{2,3,1,0:T(8,128)(2,1)}, u32[]{:S(2)}) copy-start(bf16[3,16,128,128]{2,3,1,0:T(8,128)(2,1)} %copy-done.2) | copy-start | bytes 4718596
  688.3 157.3 %all-to-all-start.4 = ((bf16[32,128,512]{2,1,0:T(8,128)(2,1)}), bf16[32,128,512]{2,1,0:T(8,128)(2,1)}, u32[]{:S(2)}, u32[]{:S(2)}) async-start(bf16[32,128,512]{2,1,0:T(8,128)(2,1)} %pad_maximum_fusion.1), calls=%async_computation.4 | async-start | bytes 8388608 | tf_op jit(solution)/shard_map/all_to_all | solution.py:185
  698.2 7.5 copy-start.1
  708.3 4.8 copy-start.8
  820.9 14.8 %copy-start.71 = (s32[8]{0:T(128)S(1)}, s32[8]{0:T(128)}, u32[]{:S(2)}) copy-start(s32[8]{0:T(128)} %copy-done.70) | copy-start | bytes 100
  839.7 4.6 copy-start.48
  845.6 4.7 copy-start.49
  845.6 4.7 copy-start.50
  (37 other events, 89.2 us)
Sparse Core Ops, SparseCore 0:
  10.6 123.0 all-gather.4
  136.3 116.7 all-gather.6
where the time goes:
time: 874 us; the launch traced here: 859 us
  other arithmetic  280 us (32%)
  local copies, waits for them, and re-layouts  247 us (28%)
  waiting for transfers between devices  158 us (18%)
  matrix products  120 us (14%)
  starting transfers between devices  37.9 us (4%)
  between operations  15.9 us (2%)
    scatter-add x24, other arithmetic, spread(): total.at[slot].add(jnp.where(chosen_pick, term, 0.0)).astype(jnp.bfloat16)  190 us
    all_gather x1, waiting for transfers between devices, per_device(): lax.all_gather(key_tiles, 'seq', axis=0, tiled=True)  92.9 us
    select_n x24, local copies, waits for them, and re-layouts, spread(): jnp.where(chosen_pick, term, 0.0)  72.8 us
    all_to_all x1, waiting for transfers between devices, per_device(): lax.all_to_all(joined(near_key_parts), 'seq', split_axis=0, concat_axis=0...  45.9 us
    gather x16, local copies, waits for them, and re-layouts, fetch(): from_near = jnp.take(columns_of(near_source), near_slot, axis=0)  36.9 us
    gather x16, local copies, waits for them, and re-layouts, fetch(): from_far = jnp.take(columns_of(far_source), far_slot, axis=0)  36.7 us
    select_n x1, other arithmetic, spread(): jnp.where(chosen_pick, term, 0.0)  32.1 us
    gather x16, local copies, waits for them, and re-layouts, fetch(): from_own = jnp.take(columns_of(own_source), own_slot, axis=0)  32 us
  transfers between devices with their start and end apart: 8, of which 4 were waited for; matrix products, arithmetic and copies ran while one was open for 47% of the time, Pallas kernels for 0%

commit v1 on v0

--- a/solution.py
+++ b/solution.py
@@ -6,6 +6,11 @@
 HEADS = 8
 HEAD_DIM = 64
 floor_score = -1e30
+
+
+def close_cubes(mine, named_axis):
+    d_next = lax.all_to_all(jnp.stack([mine] * lax.axis_size(named_axis), axis=0), named_axis, 0, 0)
+    return jnp.concatenate(d_next, axis=0)
 
 
 def locate(entry_ids, group_tiles, columns):
@@ -61,10 +66,7 @@
         ),
         axis=(0, 1),
     )
-    pieces = (
-        lax.all_gather(key_tiles, "seq", axis=0, tiled=True),
-        lax.all_gather(value_tiles, "seq", axis=0, tiled=True),
-    )
+    pieces = (close_cubes(key_tiles, "seq"), lax.all_gather(value_tiles, "seq", axis=0, tiled=True))
     span_rows = pieces[0].shape[0]
     row_at = jnp.arange(span_rows, dtype=jnp.int32)
     select = (

time: 874 us -> 1030 us (1.18)
  waiting for transfers between devices: 158 us -> 287 us
  blocking collectives: 0 us -> 19 us
  starting transfers between devices: 37.9 us -> 48.6 us
    all_gather x1, waiting for transfers between devices: 7.58 us -> 132 us  [per_device(): lax.all_gather(value_tiles, 'seq', axis=0, tiled=True)]
    all_to_all x1, waiting for transfers between devices: 0.01 us -> 94 us  [close_cubes(): lax.all_to_all(jnp.stack([mine] * lax.axis_size(named_axis), axis=0), nam...]
    all_gather x1 -> x0, waiting for transfers between devices: 92.9 us -> none  [per_device(): lax.all_gather(key_tiles, 'seq', axis=0, tiled=True)]
    all_to_all x0 -> x1, blocking collectives: none -> 19 us  [per_device(): lax.all_to_all(jnp.take(key_tiles, far_out, axis=0), 'grp', split_axis=0,...]
  transfers between devices with their start and end apart: 8 -> 7, of which waited for: 4 -> 4; matrix products, arithmetic and copies ran while one was open for 47% -> 39% of each run, Pallas kernels for 0% -> 0%
where the time goes in v1:
time: 1030 us; the launch traced here: 1020 us
  waiting for transfers between devices  287 us (28%)
  other arithmetic  277 us (27%)
  local copies, waits for them, and re-layouts  252 us (24%)
  matrix products  119 us (12%)
  starting transfers between devices  48.6 us (5%)
  blocking collectives  19 us (2%)
  between operations  15.9 us (2%)
    scatter-add x24, other arithmetic, spread(): total.at[slot].add(jnp.where(chosen_pick, term, 0.0)).astype(jnp.bfloat16)  190 us
    all_gather x1, waiting for transfers between devices, per_device(): lax.all_gather(value_tiles, 'seq', axis=0, tiled=True)  132 us
    all_to_all x1, waiting for transfers between devices, close_cubes(): lax.all_to_all(jnp.stack([mine] * lax.axis_size(named_axis), axis=0), nam...  94 us
    select_n x24, local copies, waits for them, and re-layouts, spread(): jnp.where(chosen_pick, term, 0.0)  72.8 us
    all_to_all x1, waiting for transfers between devices, per_device(): lax.all_to_all(joined(near_key_parts), 'seq', split_axis=0, concat_axis=0...  45.9 us
    gather x16, local copies, waits for them, and re-layouts, fetch(): from_far = jnp.take(columns_of(far_source), far_slot, axis=0)  36.5 us
    gather x16, local copies, waits for them, and re-layouts, fetch(): from_near = jnp.take(columns_of(near_source), near_slot, axis=0)  36.5 us
    select_n x1, other arithmetic, spread(): jnp.where(chosen_pick, term, 0.0)  32.1 us
  transfers between devices with their start and end apart: 7, of which 4 were waited for; matrix products, arithmetic and copies ran while one was open for 39% of the time, Pallas kernels for 0%

profile of v1, /device:TPU:1, one launch (start us, length us, event | category | flops | bytes accessed | tf_op | source)
XLA Modules:
  0.0 1020.2 jit_solution(17884636403731763918)
XLA Ops:
  12.9 6.8 all-to-all-start
  20.5 14.4 %all-to-all-done = bf16[8,128,512]{2,1,0:T(8,128)(2,1)S(1)} async-done(((bf16[8,128,512]{2,1,0:T(8,128)(2,1)}), bf16[8,128,512]{2,1,0:T(8,128)(2,1)S(1)}, u32[]{:S(2)}, u32[]{:S(2)}) %all-to-all-start) | async-done | bytes 1048608 | tf_op jit(solution)/shard_map/all_to_all | solution.py:85
  34.9 19.0 %all_to_all.35 = bf16[8,128,512]{2,1,0:T(8,128)(2,1)} all-to-all(bf16[8,128,512]{2,1,0:T(8,128)(2,1)S(1)} %get-tuple-element.166), channel_id=1, replica_groups=mesh['grp'=8,'seq'=32] {'grp'}, dimensions={0} | all-to-all | bytes 2097152 | tf_op jit(solution)/shard_map/all_to_all | solution.py:82
  53.9 6.1 stack.3
  60.0 11.1 %all-to-all-start.1 = ((bf16[32,3,128,512]{3,2,1,0:T(8,128)(2,1)}), bf16[32,3,128,512]{3,2,1,0:T(8,128)(2,1)}, u32[]{:S(2)}, u32[]{:S(2)}) async-start(bf16[32,3,128,512]{3,2,1,0:T(8,128)(2,1)} %stack.3), calls=%async_computation.1 | async-start | bytes 25165824 | tf_op jit(solution)/shard_map/all_to_all | solution.py:12
  157.4 132.4 %all-gather.3.cloned.1.call-done = bf16[1,96,1,128,512]{4,3,2,0,1:T(8,128)(2,1)} async-done(((bf16[1,3,1,128,512]{4,3,2,0,1:T(8,128)(2,1)}), bf16[1,96,1,128,512]{4,3,2,0,1:T(8,128)(2,1)}) %all-gather.3.cloned.1.call-update) | async-done | bytes 12582928 | tf_op jit(solution)/shard_map/all_gather | solution.py:69
  289.9 19.3 %fusion.28 = bf16[32,128,512]{2,0,1:T(8,128)(2,1)S(1)} fusion(bf16[1,96,1,128,512]{4,3,2,0,1:T(8,128)(2,1)} %all-gather.3.cloned.1.call-done, s32[96]{0:T(128)S(1)} %get-tuple-element.179, s32[96]{0:T(128)S(1)} %get-tuple-element.180, s32[32]{0:T(128)S(1)} %select_reduce_fusion), kind=kOutput, calls=%fused_computation.121 | convolution fusion | flops 404759552 | bytes 16778112 | tf_op jit(solution)/shard_map/pn,ntw->ptw/dot_general | solution.py:77
  316.3 94.0 %all-to-all-done.1 = bf16[32,3,128,512]{3,2,1,0:T(8,128)(2,1)} async-done(((bf16[32,3,128,512]{3,2,1,0:T(8,128)(2,1)}), bf16[32,3,128,512]{3,2,1,0:T(8,128)(2,1)}, u32[]{:S(2)}, u32[]{:S(2)}) %all-to-all-start.1) | async-done | bytes 12582944 | tf_op jit(solution)/shard_map/all_to_all | solution.py:12
  410.3 19.1 %fusion.25 = bf16[32,128,512]{2,0,1:T(8,128)(2,1)S(1)} fusion(bf16[96,128,512]{2,1,0:T(8,128)(2,1)} %bitcast.14, s32[96]{0:T(128)S(1)} %get-tuple-element.179, s32[96]{0:T(128)S(1)} %get-tuple-element.180, s32[32]{0:T(128)S(1)} %select_reduce_fusion), kind=kOutput, calls=%fused_computation.120 | convolution fusion | flops 404759552 | bytes 16778112 | tf_op jit(solution)/shard_map/pn,ntw->ptw/dot_general | solution.py:76
  473.6 8.8 fusion.34
  487.9 4.9 fusion.38
  492.8 6.2 fusion.17
  499.0 6.1 fusion.10
  505.1 4.0 fusion.12
  542.3 4.8 fusion.8
  566.8 32.1 %bitcast_select_fusion.18 = (f32[3,16,128,128]{2,3,1,0:T(8,128)}, f32[3,16,128,128]{2,3,1,0:T(8,128)}, f32[3,16,128,128]{2,3,1,0:T(8,128)}, f32[3,16,128,128]{2,...) fusion(f32[3,16,128,2,64]{2,4,3,1,0:T(8,128)S(1)} %copy.1019, ...), kind=kLoop, calls=%fused_computation.105 | loop fusion | flops 18874368 | bytes 100663440 | tf_op jit(solution)/shard_map/jit(_where)/select_n | solution.py:105
  602.5 7.1 scatter_fusion.11
  613.3 6.7 scatter_fusion.10
  624.4 6.7 scatter_fusion.9
  635.5 6.7 scatter_fusion.8
  644.6 5.6 all-to-all-start.4
  652.5 6.7 scatter_fusion.23
  662.9 6.7 scatter_fusion.22
  670.4 3.7 copy.1052
  674.1 6.7 scatter_fusion.21
  685.2 6.7 scatter_fusion.20
  694.3 5.1 all-to-all-start.6
  702.0 6.7 scatter_fusion.7
  712.6 6.7 scatter_fusion.6
  724.3 6.7 scatter_fusion.5
  735.9 6.7 scatter_fusion.4
  746.4 10.1 all-to-all-start.3
  759.2 6.7 scatter_fusion.19
  769.9 6.7 scatter_fusion.18
  781.6 6.7 scatter_fusion.17
  793.2 6.7 scatter_fusion.16
  803.8 45.9 %all-to-all-done.3 = bf16[32,128,512]{2,1,0:T(8,128)(2,1)} async-done(((bf16[32,128,512]{2,1,0:T(8,128)(2,1)}), bf16[32,128,512]{2,1,0:T(8,128)(2,1)}, u32[]{:S(2)}, u32[]{:S(2)}) %all-to-all-start.3) | async-done | bytes 4194336 | tf_op jit(solution)/shard_map/all_to_all | solution.py:186
  849.7 9.9 all-to-all-start.5
  880.6 10.2 %scatter_fusion.3 = f32[3,128,128]{2,1,0:T(8,128)} fusion(f32[3,128,128]{2,1,0:T(8,128)} %broadcast.259.clone, s32[48]{0:T(128)S(1)} %copy-done.42, f32[48,128,128]{2,1,0:T(8,128)S(1)} %copy.1020), kind=kCustom, calls=%fused_computation.31 | custom fusion | flops 786432 | bytes 9437376 | tf_op jit(solution)/shard_map/scatter-add | solution.py:105
  894.8 10.2 %scatter_fusion.2 = f32[3,128,128]{2,1,0:T(8,128)} fusion(f32[3,128,128]{2,1,0:T(8,128)} %broadcast.259.clone.1, s32[48]{0:T(128)S(1)} %copy-done.42, f32[48,128,128]{2,1,0:T(8,128)S(1)} %copy.1017), kind=kCustom, calls=%fused_computation.30 | custom fusion | flops 786432 | bytes 9437376 | tf_op jit(solution)/shard_map/scatter-add | solution.py:105
  909.1 10.2 %scatter_fusion.1 = f32[3,128,128]{2,1,0:T(8,128)} fusion(f32[3,128,128]{2,1,0:T(8,128)} %broadcast.259.clone.2, s32[48]{0:T(128)S(1)} %copy-done.42, f32[48,128,128]{2,1,0:T(8,128)S(1)} %copy.1014), kind=kCustom, calls=%fused_computation.29 | custom fusion | flops 786432 | bytes 9437376 | tf_op jit(solution)/shard_map/scatter-add | solution.py:105
  923.3 10.2 %scatter_fusion = f32[3,128,128]{2,1,0:T(8,128)} fusion(f32[3,128,128]{2,1,0:T(8,128)} %broadcast.259.clone.3, s32[48]{0:T(128)S(1)} %copy-done.42, f32[48,128,128]{2,1,0:T(8,128)S(1)} %copy.1011), kind=kCustom, calls=%fused_computation.28 | custom fusion | flops 786432 | bytes 9437376 | tf_op jit(solution)/shard_map/scatter-add | solution.py:105
  938.2 10.2 %scatter_fusion.15 = f32[3,128,128]{2,1,0:T(8,128)} fusion(f32[3,128,128]{2,1,0:T(8,128)} %broadcast.259.clone.4, s32[48]{0:T(128)S(1)} %copy-done.42, f32[48,128,128]{2,1,0:T(8,128)S(1)} %copy.1044), kind=kCustom, calls=%fused_computation.43 | custom fusion | flops 786432 | bytes 9437376 | tf_op jit(solution)/shard_map/scatter-add | solution.py:105
  952.4 10.2 %scatter_fusion.14 = f32[3,128,128]{2,1,0:T(8,128)} fusion(f32[3,128,128]{2,1,0:T(8,128)} %broadcast.259.clone.5, s32[48]{0:T(128)S(1)} %copy-done.42, f32[48,128,128]{2,1,0:T(8,128)S(1)} %copy.1041), kind=kCustom, calls=%fused_computation.42 | custom fusion | flops 786432 | bytes 9437376 | tf_op jit(solution)/shard_map/scatter-add | solution.py:105
  967.3 10.2 %scatter_fusion.13 = f32[3,128,128]{2,1,0:T(8,128)} fusion(f32[3,128,128]{2,1,0:T(8,128)} %broadcast.259.clone.6, s32[48]{0:T(128)S(1)} %copy-done.42, f32[48,128,128]{2,1,0:T(8,128)S(1)} %copy.1038), kind=kCustom, calls=%fused_computation.41 | custom fusion | flops 786432 | bytes 9437376 | tf_op jit(solution)/shard_map/scatter-add | solution.py:105
  982.4 10.2 %scatter_fusion.12 = f32[3,128,128]{2,1,0:T(8,128)} fusion(f32[3,128,128]{2,1,0:T(8,128)} %broadcast.259.clone.7, s32[48]{0:T(128)S(1)} %copy-done.42, f32[48,128,128]{2,1,0:T(8,128)S(1)} %copy.1035), kind=kCustom, calls=%fused_computation.40 | custom fusion | flops 786432 | bytes 9437376 | tf_op jit(solution)/shard_map/scatter-add | solution.py:105
  1001.2 4.6 fusion.23
  1007.0 4.6 fusion.21
  (376 shorter events, 335.9 us)
Async XLA Ops:
  7.2 3.9 copy-start.13
  12.9 41.0 %copy-start.12 = (bf16[1,3,1,128,512]{4,3,2,1,0:T(8,128)(2,1)S(1)}, bf16[1,3,1,128,512]{4,3,2,1,0:T(8,128)(2,1)}, u32[]{:S(2)}) copy-start(bf16[1,3,1,128,512]{4,3,2,1,0:T(8,128)(2,1)} %param.17) | copy-start | bytes 1179652
  12.9 21.9 %all-to-all-start = ((bf16[8,128,512]{2,1,0:T(8,128)(2,1)}), bf16[8,128,512]{2,1,0:T(8,128)(2,1)S(1)}, u32[]{:S(2)}, u32[]{:S(2)}) async-start(bf16[8,128,512]{2,1,0:T(8,128)(2,1)} %get-tuple-element.167), calls=%async_computation | async-start | bytes 2097152 | tf_op jit(solution)/shard_map/all_to_all | solution.py:85
  19.7 270.1 %all-gather.3.cloned.1.call-start = ((), (), s32[]{:S(2)}) async-start(), calls=%async_computation.7 | async-start | bytes 12976128 | tf_op jit(solution)/shard_map/all_gather | solution.py:69
  34.9 25.1 %copy-start.25 = (bf16[8,128,512]{2,1,0:T(8,128)(2,1)}, bf16[8,128,512]{2,1,0:T(8,128)(2,1)S(1)}, u32[]{:S(2)}) copy-start(bf16[8,128,512]{2,1,0:T(8,128)(2,1)S(1)} %all-to-all-done) | copy-start | bytes 3145732
  60.0 11.1 %copy-start.55 = (s32[768,16]{0,1:T(8,128)S(1)}, s32[768,16]{0,1:T(8,128)}, u32[]{:S(2)}) copy-start(s32[768,16]{0,1:T(8,128)} %param.20) | copy-start | bytes 147460
  60.0 11.3 %copy-start.52 = (bf16[1,3,1,128,512]{4,3,2,1,0:T(8,128)(2,1)S(1)}, bf16[1,3,1,128,512]{4,3,2,1,0:T(8,128)(2,1)}, u32[]{:S(2)}) copy-start(bf16[1,3,1,128,512]{4,3,2,1,0:T(8,128)(2,1)} %param.19) | copy-start | bytes 1179652
  60.0 12.8 %copy-start.64 = (s32[768,16]{0,1:T(8,128)S(1)}, s32[768,16]{0,1:T(8,128)}, u32[]{:S(2)}) copy-start(s32[768,16]{0,1:T(8,128)} %param.21) | copy-start | bytes 147460
  60.0 350.3 %all-to-all-start.1 = ((bf16[32,3,128,512]{3,2,1,0:T(8,128)(2,1)}), bf16[32,3,128,512]{3,2,1,0:T(8,128)(2,1)}, u32[]{:S(2)}, u32[]{:S(2)}) async-start(bf16[32,3,128,512]{3,2,1,0:T(8,128)(2,1)} %stack.3), calls=%async_computation.1 | async-start | bytes 25165824 | tf_op jit(solution)/shard_map/all_to_all | solution.py:12
  71.1 6.9 copy-start.14
  76.7 408.6 %copy-start.67 = (pred[3,16]{1,0:T(4,128)(4,1)}, pred[3,16]{1,0:T(4,128)(4,1)S(1)}, u32[]{:S(2)}) copy-start(pred[3,16]{1,0:T(4,128)(4,1)S(1)} %get-tuple-element.61) | copy-start | bytes 148
  77.2 408.0 %copy-start.65 = (pred[3,16]{1,0:T(4,128)(4,1)}, pred[3,16]{1,0:T(4,128)(4,1)S(1)}, u32[]{:S(2)}) copy-start(pred[3,16]{1,0:T(4,128)(4,1)S(1)} %get-tuple-element.69) | copy-start | bytes 148
  77.3 39.0 %copy-start.45 = (s32[48]{0:T(128)}, s32[48]{0:T(128)S(1)}, u32[]{:S(2)}) copy-start(s32[48]{0:T(128)S(1)} %reshape.883) | copy-start | bytes 580
  77.4 38.9 %copy-start.43 = (s32[48]{0:T(128)}, s32[48]{0:T(128)S(1)}, u32[]{:S(2)}) copy-start(s32[48]{0:T(128)S(1)} %reshape.877) | copy-start | bytes 580
  95.8 386.6 %copy-start.37 = (bf16[3,128,128]{1,2,0:T(8,128)(2,1)}, bf16[3,128,128]{1,2,0:T(8,128)(2,1)S(1)}, u32[]{:S(2)}) copy-start(bf16[3,128,128]{1,2,0:T(8,128)(2,1)S(1)} %copy.969) | copy-start | bytes 294916
  107.4 8.1 copy-start.53
  108.2 6.5 copy-start.54
  487.9 4.9 copy-start.47
  492.8 6.3 copy-start.15
  492.8 6.3 copy-start.16
  492.8 6.2 copy-start.30
  492.8 6.2 copy-start.48
  505.1 4.0 copy-start.36
  505.1 4.0 copy-start.57
  518.8 28.2 %copy-start.4 = (bf16[3,2,128,16,128]{2,4,3,1,0:T(8,128)(2,1)}, bf16[3,2,128,16,128]{2,4,3,1,0:T(8,128)(2,1)S(1)}, u32[]{:S(2)}) copy-start(bf16[3,2,128,16,128]{2,4,3,1,0:T(8,128)(2,1)S(1)} %fusion.5) | copy-start | bytes 9437188
  527.2 36.5 %copy-start.5 = (bf16[3,2,128,16,128]{2,4,3,1,0:T(8,128)(2,1)}, bf16[3,2,128,16,128]{2,4,3,1,0:T(8,128)(2,1)S(1)}, u32[]{:S(2)}) copy-start(bf16[3,2,128,16,128]{2,4,3,1,0:T(8,128)(2,1)S(1)} %fusion.6) | copy-start | bytes 9437188
  530.2 6.5 slice-start
  536.7 23.9 %copy-start.6 = (bf16[3,2,128,16,128]{2,4,3,1,0:T(8,128)(2,1)}, bf16[3,2,128,16,128]{2,4,3,1,0:T(8,128)(2,1)S(1)}, u32[]{:S(2)}) copy-start(bf16[3,2,128,16,128]{2,4,3,1,0:T(8,128)(2,1)S(1)} %fusion.7) | copy-start | bytes 9437188
  542.3 4.8 copy-start.40
  547.1 10.4 %copy-start.7 = (bf16[3,2,128,16,128]{2,4,3,1,0:T(8,128)(2,1)}, bf16[3,2,128,16,128]{2,4,3,1,0:T(8,128)(2,1)S(1)}, u32[]{:S(2)}) copy-start(bf16[3,2,128,16,128]{2,4,3,1,0:T(8,128)(2,1)S(1)} %fusion.8) | copy-start | bytes 9437188
  642.3 7.9 copy-start.11
  644.6 49.7 %all-to-all-start.4 = ((bf16[8,128,512]{2,1,0:T(8,128)(2,1)}), bf16[8,128,512]{2,1,0:T(8,128)(2,1)}, u32[]{:S(2)}, u32[]{:S(2)}) async-start(bf16[8,128,512]{2,1,0:T(8,128)(2,1)} %pad_maximum_fusion.2), calls=%async_computation.4 | async-start | bytes 2097152 | tf_op jit(solution)/shard_map/all_to_all | solution.py:190
  691.9 7.4 copy-start.10
  694.3 52.2 %all-to-all-start.6 = ((bf16[8,128,512]{2,1,0:T(8,128)(2,1)}), bf16[8,128,512]{2,1,0:T(8,128)(2,1)}, u32[]{:S(2)}, u32[]{:S(2)}) async-start(bf16[8,128,512]{2,1,0:T(8,128)(2,1)} %pad_maximum_fusion.3), calls=%async_computation.6 | async-start | bytes 2097152 | tf_op jit(solution)/shard_map/all_to_all | solution.py:191
  746.4 10.1 copy-start.9
  746.4 103.3 %all-to-all-start.3 = ((bf16[32,128,512]{2,1,0:T(8,128)(2,1)}), bf16[32,128,512]{2,1,0:T(8,128)(2,1)}, u32[]{:S(2)}, u32[]{:S(2)}) async-start(bf16[32,128,512]{2,1,0:T(8,128)(2,1)} %pad_maximum_fusion), calls=%async_computation.3 | async-start | bytes 8388608 | tf_op jit(solution)/shard_map/all_to_all | solution.py:186
  803.8 57.0 %copy-start.56 = (bf16[3,2,64,128]{3,2,1,0:T(8,128)(2,1)S(1)}, bf16[3,2,64,128]{3,2,1,0:T(8,128)(2,1)}, u32[]{:S(2)}) copy-start(bf16[3,2,64,128]{3,2,1,0:T(8,128)(2,1)} %get-tuple-element.172) | copy-start | bytes 294916
  803.8 57.8 %copy-start.58 = (bf16[3,2,64,128]{3,2,1,0:T(8,128)(2,1)S(1)}, bf16[3,2,64,128]{3,2,1,0:T(8,128)(2,1)}, u32[]{:S(2)}) copy-start(bf16[3,2,64,128]{3,2,1,0:T(8,128)(2,1)} %get-tuple-element.174) | copy-start | bytes 294916
  803.8 58.5 %copy-start.59 = (bf16[3,2,64,128]{3,2,1,0:T(8,128)(2,1)S(1)}, bf16[3,2,64,128]{3,2,1,0:T(8,128)(2,1)}, u32[]{:S(2)}) copy-start(bf16[3,2,64,128]{3,2,1,0:T(8,128)(2,1)} %get-tuple-element.176) | copy-start | bytes 294916
  803.8 59.3 %copy-start.60 = (bf16[3,2,64,128]{3,2,1,0:T(8,128)(2,1)S(1)}, bf16[3,2,64,128]{3,2,1,0:T(8,128)(2,1)}, u32[]{:S(2)}) copy-start(bf16[3,2,64,128]{3,2,1,0:T(8,128)(2,1)} %get-tuple-element.178) | copy-start | bytes 294916
  803.8 60.0 %copy-start.3 = (bf16[3,16,128,128]{2,3,1,0:T(8,128)(2,1)S(1)}, bf16[3,16,128,128]{2,3,1,0:T(8,128)(2,1)}, u32[]{:S(2)}) copy-start(bf16[3,16,128,128]{2,3,1,0:T(8,128)(2,1)} %copy-done.2) | copy-start | bytes 4718596
  849.7 157.3 %all-to-all-start.5 = ((bf16[32,128,512]{2,1,0:T(8,128)(2,1)}), bf16[32,128,512]{2,1,0:T(8,128)(2,1)}, u32[]{:S(2)}, u32[]{:S(2)}) async-start(bf16[32,128,512]{2,1,0:T(8,128)(2,1)} %pad_maximum_fusion.1), calls=%async_computation.5 | async-start | bytes 8388608 | tf_op jit(solution)/shard_map/all_to_all | solution.py:187
  859.7 7.5 copy-start.1
  869.8 4.8 copy-start.8
  982.4 14.8 %copy-start.70 = (s32[8]{0:T(128)S(1)}, s32[8]{0:T(128)}, u32[]{:S(2)}) copy-start(s32[8]{0:T(128)} %copy-done.69) | copy-start | bytes 100
  1001.2 4.6 copy-start.49
  1007.0 4.7 copy-start.50
  1007.0 4.7 copy-start.51
  (33 other events, 75.9 us)
Sparse Core Ops, SparseCore 0:
  23.1 266.6 all-gather.2
